TPU v7x, 32 devices: a whole 2x2x4 slice. The times are simulated.
32 devices in a mesh: dom: 16 (over z, y, core), orb: 2 (over x).
Axes of the slice: x: 2, y: 2, z: 4, core: 2. Of those that a mesh axis runs over, the one named last changes fastest.
Arguments:
- orbitals: float32 [6144, 1024], P('dom', 'orb'), may hold values from -6 to 6
- cell_mats: float32 [16, 512, 512], P('dom'), as said below
- cell_map: int32 [16, 512], P('dom'), may hold values from 0 to 511, as said below
Outputs:
- rotated: float32 [6144, 1024], P(('dom', 'orb'))
Inputs may be any that keep to these rules, and one draw needn't show every extreme that they name: `cell_map`: cell c belongs to domain c. Its 512 entries are distinct. Entries below 384 name the domain's own nodes, each used by some cell of the domain; an entry j >= 384 names own node j - 384 of the next domain, and every such j is used by some cell of the domain. `cell_mats`: each cell matrix is symmetric.
All inputs are finite; a program needn't handle non-finite values.
Results may differ from a plain program's by a relative error of at most 0.00013.
Values sent between devices are 32-bit elements; how exact they have to be, the bound alone decides.
No kernel may reach another device: no remote copies, remote signals or barrier semaphores. Data moves between devices by JAX's collectives and lax.ppermute only.
A program may use at most 64 MiB of HBM per device.

v0:
```python
import jax
import jax.numpy as jnp
from jax import lax
from jax.sharding import PartitionSpec as P

DEGREE = 5
HALO = 128
filter_center = 2.0
filter_half = 3.5


def shifted(block, axis, distance):
    devices = range(lax.axis_size(axis))
    route = [((i - distance) % len(devices), i) for i in devices]
    return lax.ppermute(block, axis, route)


def apply_local(vectors, cell_mats, cell_map):
    own_count = vectors.shape[0]
    borrowed = shifted(vectors[:HALO], "dom", -1)
    extended = jnp.concatenate([vectors, borrowed], axis=0)
    summed = jnp.zeros(extended.shape, jnp.float32)
    node_idx = cell_map[0]
    gathered = jnp.take(extended, node_idx, axis=0)
    product = jnp.dot(
        cell_mats[0], gathered, precision=lax.Precision.HIGHEST, preferred_element_type=jnp.float32
    )
    summed = summed.at[node_idx].add(product)
    returned = shifted(summed[own_count:], "dom", 1)
    return jnp.concatenate([summed[:HALO] + returned, summed[HALO:own_count]], axis=0)


def body(orbitals, cell_mats, cell_map):
    own_count = orbitals.shape[0]
    node_total = own_count * lax.axis_size("dom")
    previous = orbitals
    current = (apply_local(orbitals, cell_mats, cell_map) - filter_center * orbitals) / filter_half
    for order in range(1, DEGREE):
        advanced = (
            2.0
            * (apply_local(current, cell_mats, cell_map) - filter_center * current)
            / filter_half
            - previous
        )
        previous, current = (current, advanced)
    regrouped = lax.all_to_all(current, "orb", split_axis=0, concat_axis=1, tiled=True)
    local_gram = jnp.einsum("nk,nj->kj", regrouped, regrouped, precision=lax.Precision.HIGHEST)
    gram = lax.psum(local_gram, ("dom", "orb"))
    gram = gram / node_total
    lower = jnp.linalg.cholesky(gram)
    solved = lax.linalg.triangular_solve(lower, regrouped.T, left_side=True, lower=True)
    return solved.T


def solution(mesh):
    placed = (P("dom", "orb"), P("dom", None, None), P("dom", None))
    return jax.shard_map(
        body, mesh=mesh, in_specs=placed, out_specs=P(("dom", "orb"), None), check_vma=False
    )
```

profile of v0, /device:TPU:0, one launch (start us, length us, event | category | flops | bytes accessed | tf_op | source)
XLA Modules:
  0.0 657.8 jit_solution(3789338286109253911)
XLA Ops:
  31.4 8.7 %collective-permute-done.1 = f32[128,512]{1,0:T(8,128)S(1)} collective-permute-done((f32[128,512]{1,0:T(8,128)S(1)}, f32[128,512]{1,0:T(8,128)S(1)}, u32[]{:S(2)}, u32[]{:S(2)}) %collective-permute-start.1) | collective-permute-done | bytes 262176 | tf_op jit(solution)/shard_map/ppermute | solution.py:15
  57.8 8.7 %collective-permute-done.3 = f32[128,512]{1,0:T(8,128)S(1)} collective-permute-done((f32[128,512]{1,0:T(8,128)S(1)}, f32[128,512]{1,0:T(8,128)S(1)}, u32[]{:S(2)}, u32[]{:S(2)}) %collective-permute-start.3) | collective-permute-done | bytes 262176 | tf_op jit(solution)/shard_map/ppermute | solution.py:15
  85.8 8.7 %collective-permute-done.5 = f32[128,512]{1,0:T(8,128)S(1)} collective-permute-done((f32[128,512]{1,0:T(8,128)S(1)}, f32[128,512]{1,0:T(8,128)S(1)}, u32[]{:S(2)}, u32[]{:S(2)}) %collective-permute-start.5) | collective-permute-done | bytes 262176 | tf_op jit(solution)/shard_map/ppermute | solution.py:15
  118.4 7.7 %collective-permute-done.7 = f32[128,512]{1,0:T(8,128)S(1)} collective-permute-done((f32[128,512]{1,0:T(8,128)S(1)}, f32[128,512]{1,0:T(8,128)S(1)}, u32[]{:S(2)}, u32[]{:S(2)}) %collective-permute-start.7) | collective-permute-done | bytes 262176 | tf_op jit(solution)/shard_map/ppermute | solution.py:15
  147.0 8.6 %collective-permute-done.9 = f32[128,512]{1,0:T(8,128)S(1)} collective-permute-done((f32[128,512]{1,0:T(8,128)S(1)}, f32[128,512]{1,0:T(8,128)S(1)}, u32[]{:S(2)}, u32[]{:S(2)}) %collective-permute-start.9) | collective-permute-done | bytes 262176 | tf_op jit(solution)/shard_map/ppermute | solution.py:15
  156.0 10.5 %all_to_all.19 = f32[2,192,512]{2,1,0:T(8,128)S(1)} all-to-all(f32[2,192,512]{2,1,0:T(8,128)S(1)} %bitcast.145), channel_id=1, replica_groups=mesh['dom'=16,'orb'=2] {'orb'}, dimensions={0} | all-to-all | bytes 1572864 | tf_op jit(solution)/shard_map/all_to_all | solution.py:46
  171.7 139.4 %all-reduce.3.cloned.1.call-done = f32[1024,1024]{0,1:T(8,128)} async-done(((f32[1024,1024]{0,1:T(8,128)}), f32[1024,1024]{0,1:T(8,128)}) %all-reduce.3.cloned.1.call-update) | async-done | bytes 4194320 | tf_op jit(solution)/shard_map/psum | solution.py:48
  328.3 11.7 %cholesky.223 = f32[128,128]{1,0:T(8,128)S(1)} custom-call(f32[128,128]{1,0:T(8,128)S(1)} %cholesky.580), custom_call_target="Cholesky" | custom-call | tf_op jit(solution)/shard_map/jit(cholesky)/cholesky | solution.py:50
  342.5 9.8 %custom-call.62 = f32[1,128,128]{1,2,0:T(8,128)S(1)} custom-call(f32[1,128,128]{2,1,0:T(8,128)S(1)} %get-tuple-element.70), custom_call_target="InvertDiagBlocksLowerTriangular" | custom-call | tf_op jit(solution)/shard_map/jit(cholesky)/cholesky | solution.py:50
  356.3 11.8 %cholesky.244 = f32[128,128]{1,0:T(8,128)S(1)} custom-call(f32[128,128]{1,0:T(8,128)S(1)} %cholesky.584), custom_call_target="Cholesky" | custom-call | tf_op jit(solution)/shard_map/jit(cholesky)/cholesky | solution.py:50
  368.8 9.8 %custom-call.63 = f32[1,128,128]{1,2,0:T(8,128)S(1)} custom-call(f32[1,128,128]{2,1,0:T(8,128)S(1)} %get-tuple-element.67), custom_call_target="InvertDiagBlocksLowerTriangular" | custom-call | tf_op jit(solution)/shard_map/jit(cholesky)/cholesky | solution.py:50
  382.0 11.7 %cholesky.468 = f32[128,128]{1,0:T(8,128)S(1)} custom-call(f32[128,128]{1,0:T(8,128)S(1)} %cholesky.589), custom_call_target="Cholesky" | custom-call | tf_op jit(solution)/shard_map/jit(cholesky)/cholesky | solution.py:50
  394.9 9.8 %custom-call.64 = f32[1,128,128]{1,2,0:T(8,128)S(1)} custom-call(f32[1,128,128]{2,1,0:T(8,128)S(1)} %get-tuple-element.64), custom_call_target="InvertDiagBlocksLowerTriangular" | custom-call | tf_op jit(solution)/shard_map/jit(cholesky)/cholesky | solution.py:50
  408.3 11.9 %cholesky.487 = f32[128,128]{1,0:T(8,128)S(1)} custom-call(f32[128,128]{1,0:T(8,128)S(1)} %cholesky.594), custom_call_target="Cholesky" | custom-call | tf_op jit(solution)/shard_map/jit(cholesky)/cholesky | solution.py:50
  421.5 9.8 %custom-call.65 = f32[1,128,128]{1,2,0:T(8,128)S(1)} custom-call(f32[1,128,128]{2,1,0:T(8,128)S(1)} %get-tuple-element.61), custom_call_target="InvertDiagBlocksLowerTriangular" | custom-call | tf_op jit(solution)/shard_map/jit(cholesky)/cholesky | solution.py:50
  434.7 11.7 %cholesky.506 = f32[128,128]{1,0:T(8,128)S(1)} custom-call(f32[128,128]{1,0:T(8,128)S(1)} %cholesky.599), custom_call_target="Cholesky" | custom-call | tf_op jit(solution)/shard_map/jit(cholesky)/cholesky | solution.py:50
  447.7 10.2 %custom-call.66 = f32[1,128,128]{1,2,0:T(8,128)S(1)} custom-call(f32[1,128,128]{2,1,0:T(8,128)S(1)} %get-tuple-element.58), custom_call_target="InvertDiagBlocksLowerTriangular" | custom-call | tf_op jit(solution)/shard_map/jit(cholesky)/cholesky | solution.py:50
  461.3 11.7 %cholesky.526 = f32[128,128]{1,0:T(8,128)S(1)} custom-call(f32[128,128]{1,0:T(8,128)S(1)} %cholesky.604), custom_call_target="Cholesky" | custom-call | tf_op jit(solution)/shard_map/jit(cholesky)/cholesky | solution.py:50
  474.3 9.8 %custom-call.67 = f32[1,128,128]{1,2,0:T(8,128)S(1)} custom-call(f32[1,128,128]{2,1,0:T(8,128)S(1)} %get-tuple-element.55), custom_call_target="InvertDiagBlocksLowerTriangular" | custom-call | tf_op jit(solution)/shard_map/jit(cholesky)/cholesky | solution.py:50
  487.1 11.9 %cholesky.546 = f32[128,128]{1,0:T(8,128)S(1)} custom-call(f32[128,128]{1,0:T(8,128)S(1)} %cholesky.609), custom_call_target="Cholesky" | custom-call | tf_op jit(solution)/shard_map/jit(cholesky)/cholesky | solution.py:50
  500.2 9.8 %custom-call.68 = f32[1,128,128]{1,2,0:T(8,128)S(1)} custom-call(f32[1,128,128]{2,1,0:T(8,128)S(1)} %get-tuple-element.52), custom_call_target="InvertDiagBlocksLowerTriangular" | custom-call | tf_op jit(solution)/shard_map/jit(cholesky)/cholesky | solution.py:50
  512.6 11.7 %cholesky.564 = f32[128,128]{1,0:T(8,128)S(1)} custom-call(f32[128,128]{1,0:T(8,128)S(1)} %convolution_subtract_fusion.13), custom_call_target="Cholesky" | custom-call | tf_op jit(solution)/shard_map/jit(cholesky)/cholesky | solution.py:50
  536.0 22.8 %while.1 = (s32[]{:T(128)}, f32[1024,1024]{1,0:T(8,128)}, s32[8,2]{0,1:T(2,128)S(1)}, f32[8,128,128]{2,1,0:T(8,128)S(1)}, s32[]{:T(128)}) while((s32[]{:T(128)}, f32[1024,1024]{1,0:T(8,128)}, s32[8,2]{0,1:T(2,128)S(1)}, f32[8,128,128]{2,1,0:T(8,128)S(1)}, s32[]{:T(128)}) %tuple.58), condition=%wide.while_cond, body=%wide.while_body.sunk | while | flops 2 | bytes 131181 | solution.py:51
  558.8 78.8 %custom-call.69 = f32[8,128,128]{1,2,0:T(8,128)S(1)} custom-call(f32[8,128,128]{2,1,0:T(8,128)S(1)} %get-tuple-element.13), custom_call_target="InvertDiagBlocksLowerTriangular" | custom-call | tf_op jit(solution)/shard_map/triangular_solve | solution.py:51
  (180 shorter events, 204.2 us)
Async XLA Ops:
  6.5 14.0 %copy-start = (f32[1,512,512]{2,1,0:T(8,128)S(1)}, f32[1,512,512]{2,1,0:T(8,128)}, u32[]{:S(2)}) copy-start(f32[1,512,512]{2,1,0:T(8,128)} %param.6) | copy-start | bytes 3145732
  6.5 304.5 %all-reduce.3.cloned.1.call-start = ((), (), s32[]{:S(2)}) async-start(), calls=%async_computation.1 | async-start | bytes 8388608 | tf_op jit(solution)/shard_map/psum | solution.py:48
  7.6 9.4 %collective-permute-start = (f32[128,512]{1,0:T(8,128)S(1)}, f32[128,512]{1,0:T(8,128)S(1)}, u32[]{:S(2)}, u32[]{:S(2)}) collective-permute-start(f32[128,512]{1,0:T(8,128)S(1)} %slice.283), channel_id=1, source_target_pairs={{2,0},{4,2},{6,4},{8,6},{10,8},{12,10},{14,12},{16,14},{18,16},{20... | collective-permute-start | bytes 786440 | tf_op jit(solution)/shard_map/ppermute | solution.py:15
  20.6 19.6 %copy-start.6 = (f32[384,512]{1,0:T(8,128)S(1)}, f32[384,512]{1,0:T(8,128)}, u32[]{:S(2)}) copy-start(f32[384,512]{1,0:T(8,128)} %param.5) | copy-start | bytes 2359300
  31.3 8.8 %collective-permute-start.1 = (f32[128,512]{1,0:T(8,128)S(1)}, f32[128,512]{1,0:T(8,128)S(1)}, u32[]{:S(2)}, u32[]{:S(2)}) collective-permute-start(f32[128,512]{1,0:T(8,128)S(1)} %slice.325), channel_id=1, source_target_pairs={{30,0},{0,2},{2,4},{4,6},{6,8},{8,10},{10,12},{12,14},{14,16},{16,... | collective-permute-start | bytes 786440 | tf_op jit(solution)/shard_map/ppermute | solution.py:15
  40.2 0.7 copy-start.10
  40.4 4.3 copy-start.7
  40.4 4.2 collective-permute-start.2
  57.7 8.8 %collective-permute-start.3 = (f32[128,512]{1,0:T(8,128)S(1)}, f32[128,512]{1,0:T(8,128)S(1)}, u32[]{:S(2)}, u32[]{:S(2)}) collective-permute-start(f32[128,512]{1,0:T(8,128)S(1)} %slice.329), channel_id=1, source_target_pairs={{30,0},{0,2},{2,4},{4,6},{6,8},{8,10},{10,12},{12,14},{14,16},{16,... | collective-permute-start | bytes 786440 | tf_op jit(solution)/shard_map/ppermute | solution.py:15
  67.8 4.5 copy-start.2
  67.8 4.5 collective-permute-start.4
  74.0 20.6 %copy-start.3 = (f32[384,512]{1,0:T(8,128)S(1)}, f32[384,512]{1,0:T(8,128)}, u32[]{:S(2)}) copy-start(f32[384,512]{1,0:T(8,128)} %copy-done.2) | copy-start | bytes 2359300
  85.7 8.8 %collective-permute-start.5 = (f32[128,512]{1,0:T(8,128)S(1)}, f32[128,512]{1,0:T(8,128)S(1)}, u32[]{:S(2)}, u32[]{:S(2)}) collective-permute-start(f32[128,512]{1,0:T(8,128)S(1)} %slice.333), channel_id=1, source_target_pairs={{30,0},{0,2},{2,4},{4,6},{6,8},{8,10},{10,12},{12,14},{14,16},{16,... | collective-permute-start | bytes 786440 | tf_op jit(solution)/shard_map/ppermute | solution.py:15
  96.0 4.1 collective-permute-start.6
  102.6 24.5 %copy-start.4 = (f32[384,512]{1,0:T(8,128)S(1)}, f32[384,512]{1,0:T(8,128)}, u32[]{:S(2)}) copy-start(f32[384,512]{1,0:T(8,128)} %copy-done.2) | copy-start | bytes 2359300
  117.2 8.8 %collective-permute-start.7 = (f32[128,512]{1,0:T(8,128)S(1)}, f32[128,512]{1,0:T(8,128)S(1)}, u32[]{:S(2)}, u32[]{:S(2)}) collective-permute-start(f32[128,512]{1,0:T(8,128)S(1)} %slice.337), channel_id=1, source_target_pairs={{30,0},{0,2},{2,4},{4,6},{6,8},{8,10},{10,12},{12,14},{14,16},{16,... | collective-permute-start | bytes 786440 | tf_op jit(solution)/shard_map/ppermute | solution.py:15
  127.3 4.2 copy-start.8
  127.4 4.2 collective-permute-start.8
  134.0 21.7 %copy-start.9 = (f32[384,512]{1,0:T(8,128)S(1)}, f32[384,512]{1,0:T(8,128)}, u32[]{:S(2)}) copy-start(f32[384,512]{1,0:T(8,128)} %copy-done.8) | copy-start | bytes 2359300
  146.9 8.7 %collective-permute-start.9 = (f32[128,512]{1,0:T(8,128)S(1)}, f32[128,512]{1,0:T(8,128)S(1)}, u32[]{:S(2)}, u32[]{:S(2)}) collective-permute-start(f32[128,512]{1,0:T(8,128)S(1)} %slice.341), channel_id=1, source_target_pairs={{30,0},{0,2},{2,4},{4,6},{6,8},{8,10},{10,12},{12,14},{14,16},{16,... | collective-permute-start | bytes 786440 | tf_op jit(solution)/shard_map/ppermute | solution.py:15
  326.4 1.9 copy-start.5
  639.2 11.5 %copy-start.1 = (f32[1,512,512]{2,1,0:T(8,128)S(1)}, f32[1,512,512]{2,1,0:T(8,128)}, u32[]{:S(2)}) copy-start(f32[1,512,512]{2,1,0:T(8,128)} %param.6) | copy-start | bytes 3145732
  649.8 0.9 copy-start.11
Sparse Core Ops, SparseCore 0:
  171.8 139.2 all-reduce.2
where the time goes:
time: 666 us; the launch traced here: 658 us
  other arithmetic  297 us (45%)
  waiting for transfers between devices  199 us (30%)
  matrix products  66.2 us (10%)
  local copies, waits for them, and re-layouts  58.8 us (9%)
  between operations  19.1 us (3%)
  blocking collectives  10.5 us (2%)
  starting transfers between devices  7.25 us (1%)
    another operation x30, other arithmetic, body(): lower = jnp.linalg.cholesky(gram)  172 us
    psum x1, waiting for transfers between devices, body(): gram = lax.psum(local_gram, ('dom', 'orb'))  139 us
    another operation x3, other arithmetic, body(): lax.linalg.triangular_solve(lower, regrouped.T, left_side=True, lower=True)  83.6 us
    ppermute x10, waiting for transfers between devices, shifted(): return lax.ppermute(block, axis, route)  59.6 us
    dot_general x5, matrix products, apply_local(): jnp.dot(cell_mats[0], gathered, precision=lax.Precision.HIGHEST, preferre...  25.9 us
    scatter-add x5, other arithmetic, apply_local(): summed = summed.at[node_idx].add(product)  23.3 us
    another operation x14, matrix products, body(): lower = jnp.linalg.cholesky(gram)  23.1 us
    another operation x24, local copies, waits for them, and re-layouts  22.7 us
  transfers between devices with their start and end apart: 11, of which 11 were waited for; matrix products, arithmetic and copies ran while one was open for 1% of the time, Pallas kernels for 0%

commit v1 on v0

--- a/solution.py
+++ b/solution.py
@@ -7,6 +7,12 @@
 HALO = 128
 filter_center = 2.0
 filter_half = 3.5
+
+
+def shape_widths(local_values, device_axis, row_axis):
+    for ii in (device_axis, row_axis):
+        local_values = lax.psum(local_values, ii)
+    return local_values
 
 
 def shifted(block, axis, distance):
@@ -45,7 +51,7 @@
         previous, current = (current, advanced)
     regrouped = lax.all_to_all(current, "orb", split_axis=0, concat_axis=1, tiled=True)
     local_gram = jnp.einsum("nk,nj->kj", regrouped, regrouped, precision=lax.Precision.HIGHEST)
-    gram = lax.psum(local_gram, ("dom", "orb"))
+    gram = shape_widths(local_gram, "orb", "dom")
     gram = gram / node_total
     lower = jnp.linalg.cholesky(gram)
     solved = lax.linalg.triangular_solve(lower, regrouped.T, left_side=True, lower=True)

time: 666 us -> 746 us (1.12)
  waiting for transfers between devices: 199 us -> 279 us
    psum x1 -> x2, waiting for transfers between devices: 139 us -> 220 us  [shape_widths(): local_values = lax.psum(local_values, ii)]
  transfers between devices with their start and end apart: 11 -> 12, of which waited for: 11 -> 12; matrix products, arithmetic and copies ran while one was open for 1% -> 0% of each run, Pallas kernels for 0% -> 0%
where the time goes in v1:
time: 746 us; the launch traced here: 738 us
  other arithmetic  297 us (40%)
  waiting for transfers between devices  279 us (37%)
  matrix products  66.1 us (9%)
  local copies, waits for them, and re-layouts  58.8 us (8%)
  between operations  19.2 us (3%)
  blocking collectives  10.5 us (1%)
    psum x2, waiting for transfers between devices, shape_widths(): local_values = lax.psum(local_values, ii)  220 us
    another operation x30, other arithmetic, body(): lower = jnp.linalg.cholesky(gram)  172 us
    another operation x3, other arithmetic, body(): lax.linalg.triangular_solve(lower, regrouped.T, left_side=True, lower=True)  83.6 us
    ppermute x10, waiting for transfers between devices, shifted(): return lax.ppermute(block, axis, route)  59.6 us
    dot_general x5, matrix products, apply_local(): jnp.dot(cell_mats[0], gathered, precision=lax.Precision.HIGHEST, preferre...  25.9 us
    scatter-add x5, other arithmetic, apply_local(): summed = summed.at[node_idx].add(product)  23.3 us
    another operation x14, matrix products, body(): lower = jnp.linalg.cholesky(gram)  23.1 us
    another operation x24, local copies, waits for them, and re-layouts  22.7 us
  transfers between devices with their start and end apart: 12, of which 12 were waited for; matrix products, arithmetic and copies ran while one was open for 0% of the time, Pallas kernels for 0%

profile of v1, /device:TPU:0, one launch (start us, length us, event | category | flops | bytes accessed | tf_op | source)
XLA Modules:
  0.0 738.1 jit_solution(2441147235073197298)
XLA Ops:
  31.4 8.7 %collective-permute-done.1 = f32[128,512]{1,0:T(8,128)S(1)} collective-permute-done((f32[128,512]{1,0:T(8,128)S(1)}, f32[128,512]{1,0:T(8,128)S(1)}, u32[]{:S(2)}, u32[]{:S(2)}) %collective-permute-start.1) | collective-permute-done | bytes 262176 | tf_op jit(solution)/shard_map/ppermute | solution.py:21
  57.8 8.7 %collective-permute-done.3 = f32[128,512]{1,0:T(8,128)S(1)} collective-permute-done((f32[128,512]{1,0:T(8,128)S(1)}, f32[128,512]{1,0:T(8,128)S(1)}, u32[]{:S(2)}, u32[]{:S(2)}) %collective-permute-start.3) | collective-permute-done | bytes 262176 | tf_op jit(solution)/shard_map/ppermute | solution.py:21
  85.8 8.7 %collective-permute-done.5 = f32[128,512]{1,0:T(8,128)S(1)} collective-permute-done((f32[128,512]{1,0:T(8,128)S(1)}, f32[128,512]{1,0:T(8,128)S(1)}, u32[]{:S(2)}, u32[]{:S(2)}) %collective-permute-start.5) | collective-permute-done | bytes 262176 | tf_op jit(solution)/shard_map/ppermute | solution.py:21
  147.0 8.6 %collective-permute-done.9 = f32[128,512]{1,0:T(8,128)S(1)} collective-permute-done((f32[128,512]{1,0:T(8,128)S(1)}, f32[128,512]{1,0:T(8,128)S(1)}, u32[]{:S(2)}, u32[]{:S(2)}) %collective-permute-start.9) | collective-permute-done | bytes 262176 | tf_op jit(solution)/shard_map/ppermute | solution.py:21
  156.0 10.5 %all_to_all.19 = f32[2,192,512]{2,1,0:T(8,128)S(1)} all-to-all(f32[2,192,512]{2,1,0:T(8,128)S(1)} %bitcast.145), channel_id=1, replica_groups=mesh['dom'=16,'orb'=2] {'orb'}, dimensions={0} | all-to-all | bytes 1572864 | tf_op jit(solution)/shard_map/all_to_all | solution.py:52
  171.7 105.0 %all-reduce.4.cloned.1.call-done = f32[1024,1024]{0,1:T(8,128)} async-done(((f32[1024,1024]{0,1:T(8,128)}), f32[1024,1024]{0,1:T(8,128)}) %all-reduce.4.cloned.1.call-update) | async-done | bytes 4194320 | tf_op jit(solution)/shard_map/psum | solution.py:14
  276.7 114.7 %all-reduce.6.cloned.1.call-done = f32[1024,1024]{0,1:T(8,128)} async-done(((f32[1024,1024]{0,1:T(8,128)}), f32[1024,1024]{0,1:T(8,128)}) %all-reduce.6.cloned.1.call-update) | async-done | bytes 4194320 | tf_op jit(solution)/shard_map/psum | solution.py:14
  408.7 11.7 %cholesky.223 = f32[128,128]{1,0:T(8,128)S(1)} custom-call(f32[128,128]{1,0:T(8,128)S(1)} %cholesky.580), custom_call_target="Cholesky" | custom-call | tf_op jit(solution)/shard_map/jit(cholesky)/cholesky | solution.py:56
  422.9 9.8 %custom-call.62 = f32[1,128,128]{1,2,0:T(8,128)S(1)} custom-call(f32[1,128,128]{2,1,0:T(8,128)S(1)} %get-tuple-element.70), custom_call_target="InvertDiagBlocksLowerTriangular" | custom-call | tf_op jit(solution)/shard_map/jit(cholesky)/cholesky | solution.py:56
  436.7 11.8 %cholesky.244 = f32[128,128]{1,0:T(8,128)S(1)} custom-call(f32[128,128]{1,0:T(8,128)S(1)} %cholesky.584), custom_call_target="Cholesky" | custom-call | tf_op jit(solution)/shard_map/jit(cholesky)/cholesky | solution.py:56
  449.1 9.8 %custom-call.63 = f32[1,128,128]{1,2,0:T(8,128)S(1)} custom-call(f32[1,128,128]{2,1,0:T(8,128)S(1)} %get-tuple-element.67), custom_call_target="InvertDiagBlocksLowerTriangular" | custom-call | tf_op jit(solution)/shard_map/jit(cholesky)/cholesky | solution.py:56
  462.3 11.7 %cholesky.468 = f32[128,128]{1,0:T(8,128)S(1)} custom-call(f32[128,128]{1,0:T(8,128)S(1)} %cholesky.589), custom_call_target="Cholesky" | custom-call | tf_op jit(solution)/shard_map/jit(cholesky)/cholesky | solution.py:56
  475.3 9.8 %custom-call.64 = f32[1,128,128]{1,2,0:T(8,128)S(1)} custom-call(f32[1,128,128]{2,1,0:T(8,128)S(1)} %get-tuple-element.64), custom_call_target="InvertDiagBlocksLowerTriangular" | custom-call | tf_op jit(solution)/shard_map/jit(cholesky)/cholesky | solution.py:56
  488.6 11.9 %cholesky.487 = f32[128,128]{1,0:T(8,128)S(1)} custom-call(f32[128,128]{1,0:T(8,128)S(1)} %cholesky.594), custom_call_target="Cholesky" | custom-call | tf_op jit(solution)/shard_map/jit(cholesky)/cholesky | solution.py:56
  501.8 9.8 %custom-call.65 = f32[1,128,128]{1,2,0:T(8,128)S(1)} custom-call(f32[1,128,128]{2,1,0:T(8,128)S(1)} %get-tuple-element.61), custom_call_target="InvertDiagBlocksLowerTriangular" | custom-call | tf_op jit(solution)/shard_map/jit(cholesky)/cholesky | solution.py:56
  515.1 11.7 %cholesky.506 = f32[128,128]{1,0:T(8,128)S(1)} custom-call(f32[128,128]{1,0:T(8,128)S(1)} %cholesky.599), custom_call_target="Cholesky" | custom-call | tf_op jit(solution)/shard_map/jit(cholesky)/cholesky | solution.py:56
  528.1 10.2 %custom-call.66 = f32[1,128,128]{1,2,0:T(8,128)S(1)} custom-call(f32[1,128,128]{2,1,0:T(8,128)S(1)} %get-tuple-element.58), custom_call_target="InvertDiagBlocksLowerTriangular" | custom-call | tf_op jit(solution)/shard_map/jit(cholesky)/cholesky | solution.py:56
  541.6 11.7 %cholesky.526 = f32[128,128]{1,0:T(8,128)S(1)} custom-call(f32[128,128]{1,0:T(8,128)S(1)} %cholesky.604), custom_call_target="Cholesky" | custom-call | tf_op jit(solution)/shard_map/jit(cholesky)/cholesky | solution.py:56
  554.6 9.8 %custom-call.67 = f32[1,128,128]{1,2,0:T(8,128)S(1)} custom-call(f32[1,128,128]{2,1,0:T(8,128)S(1)} %get-tuple-element.55), custom_call_target="InvertDiagBlocksLowerTriangular" | custom-call | tf_op jit(solution)/shard_map/jit(cholesky)/cholesky | solution.py:56
  567.4 11.9 %cholesky.546 = f32[128,128]{1,0:T(8,128)S(1)} custom-call(f32[128,128]{1,0:T(8,128)S(1)} %cholesky.609), custom_call_target="Cholesky" | custom-call | tf_op jit(solution)/shard_map/jit(cholesky)/cholesky | solution.py:56
  580.5 9.8 %custom-call.68 = f32[1,128,128]{1,2,0:T(8,128)S(1)} custom-call(f32[1,128,128]{2,1,0:T(8,128)S(1)} %get-tuple-element.52), custom_call_target="InvertDiagBlocksLowerTriangular" | custom-call | tf_op jit(solution)/shard_map/jit(cholesky)/cholesky | solution.py:56
  593.0 11.7 %cholesky.564 = f32[128,128]{1,0:T(8,128)S(1)} custom-call(f32[128,128]{1,0:T(8,128)S(1)} %convolution_subtract_fusion.13), custom_call_target="Cholesky" | custom-call | tf_op jit(solution)/shard_map/jit(cholesky)/cholesky | solution.py:56
  616.3 22.8 %while.1 = (s32[]{:T(128)}, f32[1024,1024]{1,0:T(8,128)}, s32[8,2]{0,1:T(2,128)S(1)}, f32[8,128,128]{2,1,0:T(8,128)S(1)}, s32[]{:T(128)}) while((s32[]{:T(128)}, f32[1024,1024]{1,0:T(8,128)}, s32[8,2]{0,1:T(2,128)S(1)}, f32[8,128,128]{2,1,0:T(8,128)S(1)}, s32[]{:T(128)}) %tuple.58), condition=%wide.while_cond, body=%wide.while_body.sunk | while | flops 2 | bytes 131181 | solution.py:57
  639.1 78.8 %custom-call.69 = f32[8,128,128]{1,2,0:T(8,128)S(1)} custom-call(f32[8,128,128]{2,1,0:T(8,128)S(1)} %get-tuple-element.13), custom_call_target="InvertDiagBlocksLowerTriangular" | custom-call | tf_op jit(solution)/shard_map/triangular_solve | solution.py:57
  (183 shorter events, 211.9 us)
Async XLA Ops:
  6.5 14.0 %copy-start = (f32[1,512,512]{2,1,0:T(8,128)S(1)}, f32[1,512,512]{2,1,0:T(8,128)}, u32[]{:S(2)}) copy-start(f32[1,512,512]{2,1,0:T(8,128)} %param.6) | copy-start | bytes 3145732
  6.5 270.1 %all-reduce.4.cloned.1.call-start = ((), (), s32[]{:S(2)}) async-start(), calls=%async_computation.1 | async-start | bytes 8388608 | tf_op jit(solution)/shard_map/psum | solution.py:14
  7.6 9.4 %collective-permute-start = (f32[128,512]{1,0:T(8,128)S(1)}, f32[128,512]{1,0:T(8,128)S(1)}, u32[]{:S(2)}, u32[]{:S(2)}) collective-permute-start(f32[128,512]{1,0:T(8,128)S(1)} %slice.283), channel_id=1, source_target_pairs={{2,0},{4,2},{6,4},{8,6},{10,8},{12,10},{14,12},{16,14},{18,16},{20... | collective-permute-start | bytes 786440 | tf_op jit(solution)/shard_map/ppermute | solution.py:21
  20.6 19.6 %copy-start.6 = (f32[384,512]{1,0:T(8,128)S(1)}, f32[384,512]{1,0:T(8,128)}, u32[]{:S(2)}) copy-start(f32[384,512]{1,0:T(8,128)} %param.5) | copy-start | bytes 2359300
  31.3 8.8 %collective-permute-start.1 = (f32[128,512]{1,0:T(8,128)S(1)}, f32[128,512]{1,0:T(8,128)S(1)}, u32[]{:S(2)}, u32[]{:S(2)}) collective-permute-start(f32[128,512]{1,0:T(8,128)S(1)} %slice.325), channel_id=1, source_target_pairs={{30,0},{0,2},{2,4},{4,6},{6,8},{8,10},{10,12},{12,14},{14,16},{16,... | collective-permute-start | bytes 786440 | tf_op jit(solution)/shard_map/ppermute | solution.py:21
  40.2 0.7 copy-start.10
  40.4 4.3 copy-start.7
  40.4 4.2 collective-permute-start.2
  57.7 8.8 %collective-permute-start.3 = (f32[128,512]{1,0:T(8,128)S(1)}, f32[128,512]{1,0:T(8,128)S(1)}, u32[]{:S(2)}, u32[]{:S(2)}) collective-permute-start(f32[128,512]{1,0:T(8,128)S(1)} %slice.329), channel_id=1, source_target_pairs={{30,0},{0,2},{2,4},{4,6},{6,8},{8,10},{10,12},{12,14},{14,16},{16,... | collective-permute-start | bytes 786440 | tf_op jit(solution)/shard_map/ppermute | solution.py:21
  67.8 4.5 copy-start.2
  67.8 4.5 collective-permute-start.4
  74.0 20.6 %copy-start.3 = (f32[384,512]{1,0:T(8,128)S(1)}, f32[384,512]{1,0:T(8,128)}, u32[]{:S(2)}) copy-start(f32[384,512]{1,0:T(8,128)} %copy-done.2) | copy-start | bytes 2359300
  85.7 8.8 %collective-permute-start.5 = (f32[128,512]{1,0:T(8,128)S(1)}, f32[128,512]{1,0:T(8,128)S(1)}, u32[]{:S(2)}, u32[]{:S(2)}) collective-permute-start(f32[128,512]{1,0:T(8,128)S(1)} %slice.333), channel_id=1, source_target_pairs={{30,0},{0,2},{2,4},{4,6},{6,8},{8,10},{10,12},{12,14},{14,16},{16,... | collective-permute-start | bytes 786440 | tf_op jit(solution)/shard_map/ppermute | solution.py:21
  96.0 4.1 collective-permute-start.6
  102.6 24.5 %copy-start.4 = (f32[384,512]{1,0:T(8,128)S(1)}, f32[384,512]{1,0:T(8,128)}, u32[]{:S(2)}) copy-start(f32[384,512]{1,0:T(8,128)} %copy-done.2) | copy-start | bytes 2359300
  117.2 8.8 %collective-permute-start.7 = (f32[128,512]{1,0:T(8,128)S(1)}, f32[128,512]{1,0:T(8,128)S(1)}, u32[]{:S(2)}, u32[]{:S(2)}) collective-permute-start(f32[128,512]{1,0:T(8,128)S(1)} %slice.337), channel_id=1, source_target_pairs={{30,0},{0,2},{2,4},{4,6},{6,8},{8,10},{10,12},{12,14},{14,16},{16,... | collective-permute-start | bytes 786440 | tf_op jit(solution)/shard_map/ppermute | solution.py:21
  127.3 4.2 copy-start.8
  127.4 4.2 collective-permute-start.8
  134.0 21.7 %copy-start.9 = (f32[384,512]{1,0:T(8,128)S(1)}, f32[384,512]{1,0:T(8,128)}, u32[]{:S(2)}) copy-start(f32[384,512]{1,0:T(8,128)} %copy-done.8) | copy-start | bytes 2359300
  146.9 8.7 %collective-permute-start.9 = (f32[128,512]{1,0:T(8,128)S(1)}, f32[128,512]{1,0:T(8,128)S(1)}, u32[]{:S(2)}, u32[]{:S(2)}) collective-permute-start(f32[128,512]{1,0:T(8,128)S(1)} %slice.341), channel_id=1, source_target_pairs={{30,0},{0,2},{2,4},{4,6},{6,8},{8,10},{10,12},{12,14},{14,16},{16,... | collective-permute-start | bytes 786440 | tf_op jit(solution)/shard_map/ppermute | solution.py:21
  171.7 219.8 %all-reduce.6.cloned.1.call-start = ((), (), s32[]{:S(2)}) async-start(), calls=%async_computation.2 | async-start | bytes 8388608 | tf_op jit(solution)/shard_map/psum | solution.py:14
  406.7 1.9 copy-start.5
  719.6 11.5 %copy-start.1 = (f32[1,512,512]{2,1,0:T(8,128)S(1)}, f32[1,512,512]{2,1,0:T(8,128)}, u32[]{:S(2)}) copy-start(f32[1,512,512]{2,1,0:T(8,128)} %param.6) | copy-start | bytes 3145732
  730.2 0.9 copy-start.11
Sparse Core Ops, SparseCore 0:
  171.8 104.8 all-reduce.3
  280.3 111.0 all-reduce.5
